TPU v7x, 256 devices: a whole 4x4x8 slice. The times are simulated.
256 devices in a mesh: feat: 16 (over z, y_lo), cand: 16 (over x, y_hi, core).
Axes of the slice: x: 4, y: 4 (y_hi: 2, y_lo: 2; y = y_hi * 2 + y_lo), z: 8, core: 2. Of those that a mesh axis runs over, the one named last changes fastest.
Arguments:
- cand_grads: bfloat16 [1024, 1048576], P('cand', 'feat'), may hold values from -30 to 30
- val_grads: bfloat16 [256, 1048576], P('cand', 'feat'), may hold values from -30 to 30
- second_moment: float32 [1048576], P('feat'), may hold values from 0.0005 to 1.5
- slot_blocks: int32 [8, 128], replicated, may hold values from 0 to 127, as said below
- slot_seeds: int32 [8, 128], replicated, may hold values from 0 to 1073741823
Outputs:
- scores: float32 [1024, 64], P('cand', 'feat')
Inputs may be any that keep to these rules, and one draw needn't show every extreme that they name: `slot_blocks`: each row is a permutation of the input blocks; with L = 128 / (devices of feat), G = (devices of feat) / 8, and o_k = k * G for even k and (k - 1) * G + 1 for odd k, slot k of output block b reads an input block whose index divided by L equals (b / L + o_k) modulo the devices of feat (divisions rounded down).
All inputs are finite; a program needn't handle non-finite values.
Results may differ from a plain program's by a relative error of at most 0.0003.
Values sent between devices are 32-bit elements; how exact they have to be, the bound alone decides.
No kernel may reach another device: no remote copies, remote signals or barrier semaphores. Data moves between devices by JAX's collectives and lax.ppermute only.
A program may use at most 64 MiB of HBM per device.

v0:
```python
import math
import jax
import jax.numpy as jnp
from jax import lax
from jax.sharding import PartitionSpec as P

PB = 8192
FEATS = 8192
FB = 64
SLOTS = 8
VPT = 4


def block_signs(seed_val, height, breadth):
    across = lax.broadcasted_iota(jnp.int32, (height, breadth), 0)
    column = lax.broadcasted_iota(jnp.int32, (height, breadth), 1)
    mixed = seed_val ^ across * jnp.int32(73856093) ^ column * jnp.int32(19349663)
    for repeat in range(2):
        mixed = mixed ^ lax.shift_right_logical(mixed, jnp.int32(16))
        mixed = mixed * jnp.int32(73244475)
    mixed = mixed ^ lax.shift_right_logical(mixed, jnp.int32(16))
    return (2 * (mixed & 1) - 1).astype(jnp.float32)


def signs_for(seed_val):
    return block_signs(seed_val, PB, FB)


def squares(features):
    return jnp.sum(features * features, axis=(0, 2))


def body(cand_grads, val_grads, second_moment, slot_blocks, slot_seeds):
    local_blocks = second_moment.shape[0] // PB
    first_block = lax.axis_index("feat") * local_blocks
    groups = FEATS // 128
    per_group = 128 // FB
    factor = 1.0 / math.sqrt(SLOTS * PB)
    ncand = cand_grads.shape[0]
    wide = cand_grads.astype(jnp.float32)
    adam_grads = (
        wide / (jnp.sqrt(0.999 * second_moment[None, :] + 0.001 * wide * wide) + 1e-08)
    ).astype(jnp.bfloat16)
    rows_all = jnp.concatenate([adam_grads, val_grads], axis=0)
    height = rows_all.shape[0]

    def one_block(position, summed):
        segment = lax.dynamic_slice_in_dim(rows_all, position * PB, PB, 1)
        matches = (slot_blocks == first_block + position).astype(jnp.int32)
        seeds_now = jnp.sum(slot_seeds * matches, axis=1)
        matrices = (jax.vmap(signs_for)(seeds_now) * factor).astype(jnp.bfloat16)
        partial_out = jnp.einsum(
            "rp,kpf->rkf", segment, matrices, preferred_element_type=jnp.float32
        )
        placing = matches.astype(jnp.float32).reshape(SLOTS, groups, per_group)
        return summed + jnp.einsum(
            "rkf,kgh->grhf", partial_out, placing, precision=lax.Precision.HIGHEST
        )

    start_sum = jnp.zeros((groups, height, per_group, FB), jnp.float32)
    summed = lax.fori_loop(0, local_blocks, one_block, start_sum)
    mine = lax.psum_scatter(
        summed.reshape(groups, height, 128), "feat", scatter_dimension=0, tiled=True
    )
    cand_part = mine[:, :ncand, :]
    val_part = mine[:, ncand:, :]
    cand_sq, val_sq = lax.psum((squares(cand_part), squares(val_part)), "feat")
    val_unit = val_part / jnp.sqrt(val_sq + 1e-06)[None, :, None]
    val_all = lax.all_gather(val_unit, "cand", axis=1, tiled=True)
    dots = jnp.einsum("gih,gvh->iv", cand_part, val_all, precision=lax.Precision.HIGHEST)
    tile = jnp.sum(dots.reshape(ncand, -1, VPT), axis=2) / VPT
    total = lax.psum(tile, "feat")
    width_own = total.shape[1] // lax.axis_size("feat")
    owned = lax.dynamic_slice_in_dim(total, lax.axis_index("feat") * width_own, width_own, 1)
    cand_norm = jnp.sqrt(cand_sq + 1e-06)
    return owned / cand_norm[:, None]


def solution(mesh):
    placed = (P("cand", "feat"), P("cand", "feat"), P("feat"), P(), P())
    return jax.shard_map(
        body, mesh=mesh, in_specs=placed, out_specs=P("cand", "feat"), check_vma=False
    )
```

profile of v0, /device:TPU:0, one launch (start us, length us, event | category | flops | bytes accessed | tf_op | source)
XLA Modules:
  0.0 388.0 jit_solution(3409171600617798099)
XLA Ops:
  6.5 0.0 copy-start
  6.5 0.0 reduce-scatter.2.cloned.1.call-start
  6.5 1.1 broadcast_multiply_fusion
  7.7 0.8 copy.16
  8.5 0.8 copy.17
  9.2 9.5 %fusion.14 = bf16[64,65536]{1,0:T(8,128)(2,1)S(1)} fusion(bf16[64,65536]{1,0:T(8,128)(2,1)} %param.7, f32[65536]{0:T(1024)S(1)} %broadcast_multiply_fusion), kind=kLoop, calls=%fused_computation.25 | loop fusion | flops 29360128 | bytes 17039360 | tf_op jit(solution)/shard_map/convert_element_type | solution.py:43
  18.8 0.0 copy-done
  18.8 6.3 %pad_maximum_fusion = bf16[80,65536]{1,0:T(8,128)(2,1)} fusion(bf16[16,65536]{1,0:T(8,128)(2,1)S(1)} %copy-done, bf16[64,65536]{1,0:T(8,128)(2,1)S(1)} %fusion.14), kind=kLoop, calls=%fused_computation.29 | loop fusion | flops 20971520 | bytes 20971520 | tf_op jit(solution)/shard_map/concatenate | solution.py:44
  25.1 148.3 %while.16 = (s32[]{:T(128)}, f32[64,80,2,64]{1,0,3,2:T(8,128)}, s32[]{:T(128)}, s32[8,128]{0,1:T(8,128)S(1)}, bf16[80,65536]{1,0:T(8,128)(2,1)}, /*index=5*/s32[...) while((s32[]{:T(128)}, f32[64,80,2,64]{1,0,3,2:T(8,128)}, s32[]{:T(128)}, ...), condition=%wide.region_2.0_spmd.clone, body=%wide.region_0.0_spmd.clone.sunk | while | flops 802436160 | bytes 23841520 | solution.py:61
  25.2 8.3 %fusion.32 = bf16[8,8192,64]{1,2,0:T(8,128)(2,1)S(1)} fusion(s32[64]{0:T(128)S(1)} %iota_multiply_fusion.4, s32[8192]{0:T(1024)S(1)} %iota_multiply_fusion.5, s32[8]{0:T(128)S(1)} %select_reduce_fusion.2), kind=kLoop, calls=%fused_computation.10.clone.1 | loop fusion | flops 67108864 | bytes 8421664 | tf_op jit(solution)/shard_map/while/body/eval_jaxpr/convert_element_type | solution.py:51
  33.5 3.7 fusion.33
  37.2 5.1 %bitcast_add_fusion.2 = f32[64,80,2,64]{1,0,3,2:T(8,128)} fusion(f32[64,80,2,64]{1,0,3,2:T(8,128)} %get-tuple-element.261, pred[]{:T(512)S(6)} %compare.3, f32[80,8,64]{0,2,1:T(8,128)S(1)} %bitcast.32, f32[8,64,2,1]{0,2,1,3:T(2,128)S(1)} %bitcast.33), kind=kOutput, calls=%fused_computation.11.clone.1 | convolution fusion | flops 64225280 | bytes 5410817 | tf_op jit(solution)/shard_map/while/body/eval_jaxpr/rkf,kgh->grhf/dot_general | solution.py:56
  42.3 8.3 %fusion.32 = bf16[8,8192,64]{1,2,0:T(8,128)(2,1)S(1)} fusion(s32[64]{0:T(128)S(1)} %iota_multiply_fusion.4, s32[8192]{0:T(1024)S(1)} %iota_multiply_fusion.5, s32[8]{0:T(128)S(1)} %select_reduce_fusion.2), kind=kLoop, calls=%fused_computation.10.clone.1 | loop fusion | flops 67108864 | bytes 8421664 | tf_op jit(solution)/shard_map/while/body/eval_jaxpr/convert_element_type | solution.py:51
  50.7 3.7 fusion.33
  54.4 6.6 %bitcast_add_fusion.2 = f32[64,80,2,64]{1,0,3,2:T(8,128)} fusion(f32[64,80,2,64]{1,0,3,2:T(8,128)} %get-tuple-element.261, pred[]{:T(512)S(6)} %compare.3, f32[80,8,64]{0,2,1:T(8,128)S(1)} %bitcast.32, f32[8,64,2,1]{0,2,1,3:T(2,128)S(1)} %bitcast.33), kind=kOutput, calls=%fused_computation.11.clone.1 | convolution fusion | flops 64225280 | bytes 5410817 | tf_op jit(solution)/shard_map/while/body/eval_jaxpr/rkf,kgh->grhf/dot_general | solution.py:56
  61.1 8.3 %fusion.32 = bf16[8,8192,64]{1,2,0:T(8,128)(2,1)S(1)} fusion(s32[64]{0:T(128)S(1)} %iota_multiply_fusion.4, s32[8192]{0:T(1024)S(1)} %iota_multiply_fusion.5, s32[8]{0:T(128)S(1)} %select_reduce_fusion.2), kind=kLoop, calls=%fused_computation.10.clone.1 | loop fusion | flops 67108864 | bytes 8421664 | tf_op jit(solution)/shard_map/while/body/eval_jaxpr/convert_element_type | solution.py:51
  69.4 3.7 fusion.33
  73.1 6.6 %bitcast_add_fusion.2 = f32[64,80,2,64]{1,0,3,2:T(8,128)} fusion(f32[64,80,2,64]{1,0,3,2:T(8,128)} %get-tuple-element.261, pred[]{:T(512)S(6)} %compare.3, f32[80,8,64]{0,2,1:T(8,128)S(1)} %bitcast.32, f32[8,64,2,1]{0,2,1,3:T(2,128)S(1)} %bitcast.33), kind=kOutput, calls=%fused_computation.11.clone.1 | convolution fusion | flops 64225280 | bytes 5410817 | tf_op jit(solution)/shard_map/while/body/eval_jaxpr/rkf,kgh->grhf/dot_general | solution.py:56
  79.8 8.3 %fusion.32 = bf16[8,8192,64]{1,2,0:T(8,128)(2,1)S(1)} fusion(s32[64]{0:T(128)S(1)} %iota_multiply_fusion.4, s32[8192]{0:T(1024)S(1)} %iota_multiply_fusion.5, s32[8]{0:T(128)S(1)} %select_reduce_fusion.2), kind=kLoop, calls=%fused_computation.10.clone.1 | loop fusion | flops 67108864 | bytes 8421664 | tf_op jit(solution)/shard_map/while/body/eval_jaxpr/convert_element_type | solution.py:51
  88.1 3.7 fusion.33
  91.8 6.6 %bitcast_add_fusion.2 = f32[64,80,2,64]{1,0,3,2:T(8,128)} fusion(f32[64,80,2,64]{1,0,3,2:T(8,128)} %get-tuple-element.261, pred[]{:T(512)S(6)} %compare.3, f32[80,8,64]{0,2,1:T(8,128)S(1)} %bitcast.32, f32[8,64,2,1]{0,2,1,3:T(2,128)S(1)} %bitcast.33), kind=kOutput, calls=%fused_computation.11.clone.1 | convolution fusion | flops 64225280 | bytes 5410817 | tf_op jit(solution)/shard_map/while/body/eval_jaxpr/rkf,kgh->grhf/dot_general | solution.py:56
  98.5 8.3 %fusion.32 = bf16[8,8192,64]{1,2,0:T(8,128)(2,1)S(1)} fusion(s32[64]{0:T(128)S(1)} %iota_multiply_fusion.4, s32[8192]{0:T(1024)S(1)} %iota_multiply_fusion.5, s32[8]{0:T(128)S(1)} %select_reduce_fusion.2), kind=kLoop, calls=%fused_computation.10.clone.1 | loop fusion | flops 67108864 | bytes 8421664 | tf_op jit(solution)/shard_map/while/body/eval_jaxpr/convert_element_type | solution.py:51
  106.9 3.7 fusion.33
  110.6 6.6 %bitcast_add_fusion.2 = f32[64,80,2,64]{1,0,3,2:T(8,128)} fusion(f32[64,80,2,64]{1,0,3,2:T(8,128)} %get-tuple-element.261, pred[]{:T(512)S(6)} %compare.3, f32[80,8,64]{0,2,1:T(8,128)S(1)} %bitcast.32, f32[8,64,2,1]{0,2,1,3:T(2,128)S(1)} %bitcast.33), kind=kOutput, calls=%fused_computation.11.clone.1 | convolution fusion | flops 64225280 | bytes 5410817 | tf_op jit(solution)/shard_map/while/body/eval_jaxpr/rkf,kgh->grhf/dot_general | solution.py:56
  117.3 8.3 %fusion.32 = bf16[8,8192,64]{1,2,0:T(8,128)(2,1)S(1)} fusion(s32[64]{0:T(128)S(1)} %iota_multiply_fusion.4, s32[8192]{0:T(1024)S(1)} %iota_multiply_fusion.5, s32[8]{0:T(128)S(1)} %select_reduce_fusion.2), kind=kLoop, calls=%fused_computation.10.clone.1 | loop fusion | flops 67108864 | bytes 8421664 | tf_op jit(solution)/shard_map/while/body/eval_jaxpr/convert_element_type | solution.py:51
  125.6 3.7 fusion.33
  129.3 6.6 %bitcast_add_fusion.2 = f32[64,80,2,64]{1,0,3,2:T(8,128)} fusion(f32[64,80,2,64]{1,0,3,2:T(8,128)} %get-tuple-element.261, pred[]{:T(512)S(6)} %compare.3, f32[80,8,64]{0,2,1:T(8,128)S(1)} %bitcast.32, f32[8,64,2,1]{0,2,1,3:T(2,128)S(1)} %bitcast.33), kind=kOutput, calls=%fused_computation.11.clone.1 | convolution fusion | flops 64225280 | bytes 5410817 | tf_op jit(solution)/shard_map/while/body/eval_jaxpr/rkf,kgh->grhf/dot_general | solution.py:56
  136.0 8.3 %fusion.32 = bf16[8,8192,64]{1,2,0:T(8,128)(2,1)S(1)} fusion(s32[64]{0:T(128)S(1)} %iota_multiply_fusion.4, s32[8192]{0:T(1024)S(1)} %iota_multiply_fusion.5, s32[8]{0:T(128)S(1)} %select_reduce_fusion.2), kind=kLoop, calls=%fused_computation.10.clone.1 | loop fusion | flops 67108864 | bytes 8421664 | tf_op jit(solution)/shard_map/while/body/eval_jaxpr/convert_element_type | solution.py:51
  144.3 3.7 fusion.33
  148.0 6.6 %bitcast_add_fusion.2 = f32[64,80,2,64]{1,0,3,2:T(8,128)} fusion(f32[64,80,2,64]{1,0,3,2:T(8,128)} %get-tuple-element.261, pred[]{:T(512)S(6)} %compare.3, f32[80,8,64]{0,2,1:T(8,128)S(1)} %bitcast.32, f32[8,64,2,1]{0,2,1,3:T(2,128)S(1)} %bitcast.33), kind=kOutput, calls=%fused_computation.11.clone.1 | convolution fusion | flops 64225280 | bytes 5410817 | tf_op jit(solution)/shard_map/while/body/eval_jaxpr/rkf,kgh->grhf/dot_general | solution.py:56
  154.7 8.3 %fusion.32 = bf16[8,8192,64]{1,2,0:T(8,128)(2,1)S(1)} fusion(s32[64]{0:T(128)S(1)} %iota_multiply_fusion.4, s32[8192]{0:T(1024)S(1)} %iota_multiply_fusion.5, s32[8]{0:T(128)S(1)} %select_reduce_fusion.2), kind=kLoop, calls=%fused_computation.10.clone.1 | loop fusion | flops 67108864 | bytes 8421664 | tf_op jit(solution)/shard_map/while/body/eval_jaxpr/convert_element_type | solution.py:51
  163.1 3.7 fusion.33
  166.8 6.6 %bitcast_add_fusion.2 = f32[64,80,2,64]{1,0,3,2:T(8,128)} fusion(f32[64,80,2,64]{1,0,3,2:T(8,128)} %get-tuple-element.261, pred[]{:T(512)S(6)} %compare.3, f32[80,8,64]{0,2,1:T(8,128)S(1)} %bitcast.32, f32[8,64,2,1]{0,2,1,3:T(2,128)S(1)} %bitcast.33), kind=kOutput, calls=%fused_computation.11.clone.1 | convolution fusion | flops 64225280 | bytes 5410817 | tf_op jit(solution)/shard_map/while/body/eval_jaxpr/rkf,kgh->grhf/dot_general | solution.py:56
  173.4 5.2 %copy.19 = f32[64,80,128]{2,1,0:T(8,128)} copy(f32[64,80,128]{1,0,2:T(8,128)} %bitcast.31) | data formatting | bytes 5242880 | tf_op jit(solution)/shard_map/reshape | solution.py:63
  178.6 0.0 reduce-scatter.2.cloned.1.call-update
  178.6 79.4 %reduce-scatter.2.cloned.1.call-done = f32[4,80,128]{2,1,0:T(8,128)} async-done(((f32[64,80,128]{2,1,0:T(8,128)}), f32[4,80,128]{2,1,0:T(8,128)}) %reduce-scatter.2.cloned.1.call-update) | async-done | bytes 163856 | tf_op jit(solution)/shard_map/reduce_scatter | solution.py:62
  258.0 0.9 multiply_reduce_fusion.1
  258.9 32.8 %psum.21 = f32[16]{0:T(128)S(1)} all-reduce(f32[16]{0:T(128)S(1)} %multiply_reduce_fusion.1), channel_id=1, replica_groups=mesh['feat'=16,'cand'=16] {'feat'}, use_global_device_ids=true, to_apply=%region_5.0 | all-reduce | flops 16 | bytes 128 | tf_op jit(solution)/shard_map/psum | solution.py:67
  291.7 0.8 slice_divide_fusion
  292.5 25.5 %all_gather.3 = f32[4,256,128]{2,1,0:T(8,128)S(1)} all-gather(f32[4,16,128]{2,1,0:T(8,128)S(1)} %slice_divide_fusion), channel_id=1, replica_groups=mesh['feat'=16,'cand'=16] {'cand'}, dimensions={1}, use_global_device_ids=true | all-gather | bytes 557056 | tf_op jit(solution)/shard_map/all_gather | solution.py:69
  318.0 1.5 fusion.18
  319.5 0.1 reduce_sum.44
  319.6 1.0 multiply_reduce_fusion
  320.6 59.9 %all-reduce = (f32[64,64]{0,1:T(8,128)S(1)}, f32[64]{0:T(128)S(1)}) all-reduce(f32[64,64]{0,1:T(8,128)S(1)} %broadcast_multiply_fusion.1, f32[64]{0:T(128)S(1)} %multiply_reduce_fusion), channel_id=1, replica_groups=mesh['feat'=16,'cand'=16] {'feat'}, use_global_device_ids=true, to_apply=%region_7.0 | all-reduce | flops 4160 | bytes 33280 | tf_op jit(solution)/shard_map/psum | solution.py:72
  380.6 0.6 dynamic-slice_divide_fusion
  (36 shorter events, 0.5 us)
Async XLA Ops:
  6.5 12.2 %copy-start = (bf16[16,65536]{1,0:T(8,128)(2,1)S(1)}, bf16[16,65536]{1,0:T(8,128)(2,1)}, u32[]{:S(2)}) copy-start(bf16[16,65536]{1,0:T(8,128)(2,1)} %param.8) | copy-start | bytes 6291460
  6.5 251.5 %reduce-scatter.2.cloned.1.call-start = ((), (), s32[]{:S(2)}) async-start(), calls=%async_computation.1 | async-start | bytes 2785280 | tf_op jit(solution)/shard_map/reduce_scatter | solution.py:62
Sparse Core Ops, SparseCore 0:
  178.7 79.2 reduce-scatter.1
where the time goes:
time: 389 us; the launch traced here: 388 us
  blocking collectives  118 us (30%)
  other arithmetic  87.5 us (22%)
  matrix products  82.5 us (21%)
  waiting for transfers between devices  79.4 us (20%)
  between operations  13.4 us (3%)
  local copies, waits for them, and re-layouts  6.73 us (2%)
    reduce_scatter x1, waiting for transfers between devices, body(): lax.psum_scatter(summed.reshape(groups, height, 128), 'feat', scatter_dim...  79.4 us
    convert_element_type x8, other arithmetic, one_block(): matrices = (jax.vmap(signs_for)(seeds_now) * factor).astype(jnp.bfloat16)  66.6 us
    psum x1, blocking collectives, body(): total = lax.psum(tile, 'feat')  59.9 us
    dot_general x8, matrix products, one_block(): jnp.einsum('rkf,kgh->grhf', partial_out, placing, precision=lax.Precision...  51.4 us
    psum x1, blocking collectives, body(): cand_sq, val_sq = lax.psum((squares(cand_part), squares(val_part)), 'feat')  32.8 us
    while x8, matrix products  29.6 us
    all_gather x1, blocking collectives, body(): val_all = lax.all_gather(val_unit, 'cand', axis=1, tiled=True)  25.5 us
    convert_element_type x1, other arithmetic, body(): adam_grads = (wide / (jnp.sqrt(0.999 * second_moment[None, :] + 0.001 * w...  9.5 us
  transfers between devices with their start and end apart: 1, of which 1 were waited for; matrix products, arithmetic and copies ran while one was open for 0% of the time, Pallas kernels for 0%

commit v1 on v0

--- a/solution.py
+++ b/solution.py
@@ -69,7 +69,7 @@
     val_all = lax.all_gather(val_unit, "cand", axis=1, tiled=True)
     dots = jnp.einsum("gih,gvh->iv", cand_part, val_all, precision=lax.Precision.HIGHEST)
     tile = jnp.sum(dots.reshape(ncand, -1, VPT), axis=2) / VPT
-    total = lax.psum(tile, "feat")
+    total = jnp.sum(lax.all_gather(tile, "feat"), axis=0)
     width_own = total.shape[1] // lax.axis_size("feat")
     owned = lax.dynamic_slice_in_dim(total, lax.axis_index("feat") * width_own, width_own, 1)
     cand_norm = jnp.sqrt(cand_sq + 1e-06)

time: 389 us -> 364 us (0.936)
  blocking collectives: 118 us -> 90.8 us
    psum x1 -> x0, blocking collectives: 59.9 us -> none  [body(): total = lax.psum(tile, 'feat')]
    all_gather x0 -> x1, blocking collectives: none -> 32.4 us  [body(): total = jnp.sum(lax.all_gather(tile, 'feat'), axis=0)]
where the time goes in v1:
time: 364 us; the launch traced here: 361 us
  blocking collectives  90.8 us (25%)
  other arithmetic  87.5 us (24%)
  matrix products  82.5 us (23%)
  waiting for transfers between devices  79.4 us (22%)
  between operations  13.4 us (4%)
  local copies, waits for them, and re-layouts  6.96 us (2%)
    reduce_scatter x1, waiting for transfers between devices, body(): lax.psum_scatter(summed.reshape(groups, height, 128), 'feat', scatter_dim...  79.4 us
    convert_element_type x8, other arithmetic, one_block(): matrices = (jax.vmap(signs_for)(seeds_now) * factor).astype(jnp.bfloat16)  66.6 us
    dot_general x8, matrix products, one_block(): jnp.einsum('rkf,kgh->grhf', partial_out, placing, precision=lax.Precision...  51.4 us
    psum x1, blocking collectives, body(): cand_sq, val_sq = lax.psum((squares(cand_part), squares(val_part)), 'feat')  32.8 us
    all_gather x1, blocking collectives, body(): total = jnp.sum(lax.all_gather(tile, 'feat'), axis=0)  32.4 us
    while x8, matrix products  29.6 us
    all_gather x1, blocking collectives, body(): val_all = lax.all_gather(val_unit, 'cand', axis=1, tiled=True)  25.5 us
    convert_element_type x1, other arithmetic, body(): adam_grads = (wide / (jnp.sqrt(0.999 * second_moment[None, :] + 0.001 * w...  9.5 us
  transfers between devices with their start and end apart: 1, of which 1 were waited for; matrix products, arithmetic and copies ran while one was open for 0% of the time, Pallas kernels for 0%

profile of v1, /device:TPU:0, one launch (start us, length us, event | category | flops | bytes accessed | tf_op | source)
XLA Modules:
  0.0 360.8 jit_solution(15462680350430402034)
XLA Ops:
  6.5 0.0 copy-start
  6.5 0.0 reduce-scatter.2.cloned.1.call-start
  6.5 1.1 broadcast_multiply_fusion
  7.7 0.8 copy.40
  8.5 0.8 copy.41
  9.2 9.5 %fusion.14 = bf16[64,65536]{1,0:T(8,128)(2,1)S(1)} fusion(bf16[64,65536]{1,0:T(8,128)(2,1)} %param.7, f32[65536]{0:T(1024)S(1)} %broadcast_multiply_fusion), kind=kLoop, calls=%fused_computation.25 | loop fusion | flops 29360128 | bytes 17039360 | tf_op jit(solution)/shard_map/convert_element_type | solution.py:43
  18.8 0.0 copy-done
  18.8 6.3 %pad_maximum_fusion = bf16[80,65536]{1,0:T(8,128)(2,1)} fusion(bf16[16,65536]{1,0:T(8,128)(2,1)S(1)} %copy-done, bf16[64,65536]{1,0:T(8,128)(2,1)S(1)} %fusion.14), kind=kLoop, calls=%fused_computation.29 | loop fusion | flops 20971520 | bytes 20971520 | tf_op jit(solution)/shard_map/concatenate | solution.py:44
  25.1 148.3 %while.16 = (s32[]{:T(128)}, f32[64,80,2,64]{1,0,3,2:T(8,128)}, s32[]{:T(128)}, s32[8,128]{0,1:T(8,128)S(1)}, bf16[80,65536]{1,0:T(8,128)(2,1)}, /*index=5*/s32[...) while((s32[]{:T(128)}, f32[64,80,2,64]{1,0,3,2:T(8,128)}, s32[]{:T(128)}, ...), condition=%wide.region_2.0_spmd.clone, body=%wide.region_0.0_spmd.clone.sunk | while | flops 802436160 | bytes 23841520 | solution.py:61
  25.2 8.3 %fusion.32 = bf16[8,8192,64]{1,2,0:T(8,128)(2,1)S(1)} fusion(s32[64]{0:T(128)S(1)} %iota_multiply_fusion.4, s32[8192]{0:T(1024)S(1)} %iota_multiply_fusion.5, s32[8]{0:T(128)S(1)} %select_reduce_fusion.2), kind=kLoop, calls=%fused_computation.10.clone.1 | loop fusion | flops 67108864 | bytes 8421664 | tf_op jit(solution)/shard_map/while/body/eval_jaxpr/convert_element_type | solution.py:51
  33.5 3.7 %fusion.33 = f32[80,512]{0,1:S(1)} fusion(bf16[8192,512]{0,1:T(8,128)(2,1)S(1)} %bitcast.31, bf16[80,65536]{1,0:T(8,128)(2,1)} %get-tuple-element.292, s32[]{:T(128)S(6)} %select_n.16), kind=kOutput, calls=%fused_computation.12.clone.1 | convolution fusion | flops 671088640 | bytes 9961476 | tf_op jit(solution)/shard_map/while
  37.2 5.1 %bitcast_add_fusion.2 = f32[64,80,2,64]{1,0,3,2:T(8,128)} fusion(f32[64,80,2,64]{1,0,3,2:T(8,128)} %get-tuple-element.279, pred[]{:T(512)S(6)} %compare.3, f32[80,8,64]{0,2,1:T(8,128)S(1)} %bitcast.33, f32[8,64,2,1]{0,2,1,3:T(2,128)S(1)} %bitcast.34), kind=kOutput, calls=%fused_computation.11.clone.1 | convolution fusion | flops 64225280 | bytes 5410817 | tf_op jit(solution)/shard_map/while/body/eval_jaxpr/rkf,kgh->grhf/dot_general | solution.py:56
  42.3 8.3 %fusion.32 = bf16[8,8192,64]{1,2,0:T(8,128)(2,1)S(1)} fusion(s32[64]{0:T(128)S(1)} %iota_multiply_fusion.4, s32[8192]{0:T(1024)S(1)} %iota_multiply_fusion.5, s32[8]{0:T(128)S(1)} %select_reduce_fusion.2), kind=kLoop, calls=%fused_computation.10.clone.1 | loop fusion | flops 67108864 | bytes 8421664 | tf_op jit(solution)/shard_map/while/body/eval_jaxpr/convert_element_type | solution.py:51
  50.7 3.7 %fusion.33 = f32[80,512]{0,1:S(1)} fusion(bf16[8192,512]{0,1:T(8,128)(2,1)S(1)} %bitcast.31, bf16[80,65536]{1,0:T(8,128)(2,1)} %get-tuple-element.292, s32[]{:T(128)S(6)} %select_n.16), kind=kOutput, calls=%fused_computation.12.clone.1 | convolution fusion | flops 671088640 | bytes 9961476 | tf_op jit(solution)/shard_map/while
  54.4 6.6 %bitcast_add_fusion.2 = f32[64,80,2,64]{1,0,3,2:T(8,128)} fusion(f32[64,80,2,64]{1,0,3,2:T(8,128)} %get-tuple-element.279, pred[]{:T(512)S(6)} %compare.3, f32[80,8,64]{0,2,1:T(8,128)S(1)} %bitcast.33, f32[8,64,2,1]{0,2,1,3:T(2,128)S(1)} %bitcast.34), kind=kOutput, calls=%fused_computation.11.clone.1 | convolution fusion | flops 64225280 | bytes 5410817 | tf_op jit(solution)/shard_map/while/body/eval_jaxpr/rkf,kgh->grhf/dot_general | solution.py:56
  61.1 8.3 %fusion.32 = bf16[8,8192,64]{1,2,0:T(8,128)(2,1)S(1)} fusion(s32[64]{0:T(128)S(1)} %iota_multiply_fusion.4, s32[8192]{0:T(1024)S(1)} %iota_multiply_fusion.5, s32[8]{0:T(128)S(1)} %select_reduce_fusion.2), kind=kLoop, calls=%fused_computation.10.clone.1 | loop fusion | flops 67108864 | bytes 8421664 | tf_op jit(solution)/shard_map/while/body/eval_jaxpr/convert_element_type | solution.py:51
  69.4 3.7 %fusion.33 = f32[80,512]{0,1:S(1)} fusion(bf16[8192,512]{0,1:T(8,128)(2,1)S(1)} %bitcast.31, bf16[80,65536]{1,0:T(8,128)(2,1)} %get-tuple-element.292, s32[]{:T(128)S(6)} %select_n.16), kind=kOutput, calls=%fused_computation.12.clone.1 | convolution fusion | flops 671088640 | bytes 9961476 | tf_op jit(solution)/shard_map/while
  73.1 6.6 %bitcast_add_fusion.2 = f32[64,80,2,64]{1,0,3,2:T(8,128)} fusion(f32[64,80,2,64]{1,0,3,2:T(8,128)} %get-tuple-element.279, pred[]{:T(512)S(6)} %compare.3, f32[80,8,64]{0,2,1:T(8,128)S(1)} %bitcast.33, f32[8,64,2,1]{0,2,1,3:T(2,128)S(1)} %bitcast.34), kind=kOutput, calls=%fused_computation.11.clone.1 | convolution fusion | flops 64225280 | bytes 5410817 | tf_op jit(solution)/shard_map/while/body/eval_jaxpr/rkf,kgh->grhf/dot_general | solution.py:56
  79.8 8.3 %fusion.32 = bf16[8,8192,64]{1,2,0:T(8,128)(2,1)S(1)} fusion(s32[64]{0:T(128)S(1)} %iota_multiply_fusion.4, s32[8192]{0:T(1024)S(1)} %iota_multiply_fusion.5, s32[8]{0:T(128)S(1)} %select_reduce_fusion.2), kind=kLoop, calls=%fused_computation.10.clone.1 | loop fusion | flops 67108864 | bytes 8421664 | tf_op jit(solution)/shard_map/while/body/eval_jaxpr/convert_element_type | solution.py:51
  88.1 3.7 %fusion.33 = f32[80,512]{0,1:S(1)} fusion(bf16[8192,512]{0,1:T(8,128)(2,1)S(1)} %bitcast.31, bf16[80,65536]{1,0:T(8,128)(2,1)} %get-tuple-element.292, s32[]{:T(128)S(6)} %select_n.16), kind=kOutput, calls=%fused_computation.12.clone.1 | convolution fusion | flops 671088640 | bytes 9961476 | tf_op jit(solution)/shard_map/while
  91.8 6.6 %bitcast_add_fusion.2 = f32[64,80,2,64]{1,0,3,2:T(8,128)} fusion(f32[64,80,2,64]{1,0,3,2:T(8,128)} %get-tuple-element.279, pred[]{:T(512)S(6)} %compare.3, f32[80,8,64]{0,2,1:T(8,128)S(1)} %bitcast.33, f32[8,64,2,1]{0,2,1,3:T(2,128)S(1)} %bitcast.34), kind=kOutput, calls=%fused_computation.11.clone.1 | convolution fusion | flops 64225280 | bytes 5410817 | tf_op jit(solution)/shard_map/while/body/eval_jaxpr/rkf,kgh->grhf/dot_general | solution.py:56
  98.5 8.3 %fusion.32 = bf16[8,8192,64]{1,2,0:T(8,128)(2,1)S(1)} fusion(s32[64]{0:T(128)S(1)} %iota_multiply_fusion.4, s32[8192]{0:T(1024)S(1)} %iota_multiply_fusion.5, s32[8]{0:T(128)S(1)} %select_reduce_fusion.2), kind=kLoop, calls=%fused_computation.10.clone.1 | loop fusion | flops 67108864 | bytes 8421664 | tf_op jit(solution)/shard_map/while/body/eval_jaxpr/convert_element_type | solution.py:51
  106.9 3.7 %fusion.33 = f32[80,512]{0,1:S(1)} fusion(bf16[8192,512]{0,1:T(8,128)(2,1)S(1)} %bitcast.31, bf16[80,65536]{1,0:T(8,128)(2,1)} %get-tuple-element.292, s32[]{:T(128)S(6)} %select_n.16), kind=kOutput, calls=%fused_computation.12.clone.1 | convolution fusion | flops 671088640 | bytes 9961476 | tf_op jit(solution)/shard_map/while
  110.6 6.6 %bitcast_add_fusion.2 = f32[64,80,2,64]{1,0,3,2:T(8,128)} fusion(f32[64,80,2,64]{1,0,3,2:T(8,128)} %get-tuple-element.279, pred[]{:T(512)S(6)} %compare.3, f32[80,8,64]{0,2,1:T(8,128)S(1)} %bitcast.33, f32[8,64,2,1]{0,2,1,3:T(2,128)S(1)} %bitcast.34), kind=kOutput, calls=%fused_computation.11.clone.1 | convolution fusion | flops 64225280 | bytes 5410817 | tf_op jit(solution)/shard_map/while/body/eval_jaxpr/rkf,kgh->grhf/dot_general | solution.py:56
  117.3 8.3 %fusion.32 = bf16[8,8192,64]{1,2,0:T(8,128)(2,1)S(1)} fusion(s32[64]{0:T(128)S(1)} %iota_multiply_fusion.4, s32[8192]{0:T(1024)S(1)} %iota_multiply_fusion.5, s32[8]{0:T(128)S(1)} %select_reduce_fusion.2), kind=kLoop, calls=%fused_computation.10.clone.1 | loop fusion | flops 67108864 | bytes 8421664 | tf_op jit(solution)/shard_map/while/body/eval_jaxpr/convert_element_type | solution.py:51
  125.6 3.7 %fusion.33 = f32[80,512]{0,1:S(1)} fusion(bf16[8192,512]{0,1:T(8,128)(2,1)S(1)} %bitcast.31, bf16[80,65536]{1,0:T(8,128)(2,1)} %get-tuple-element.292, s32[]{:T(128)S(6)} %select_n.16), kind=kOutput, calls=%fused_computation.12.clone.1 | convolution fusion | flops 671088640 | bytes 9961476 | tf_op jit(solution)/shard_map/while
  129.3 6.6 %bitcast_add_fusion.2 = f32[64,80,2,64]{1,0,3,2:T(8,128)} fusion(f32[64,80,2,64]{1,0,3,2:T(8,128)} %get-tuple-element.279, pred[]{:T(512)S(6)} %compare.3, f32[80,8,64]{0,2,1:T(8,128)S(1)} %bitcast.33, f32[8,64,2,1]{0,2,1,3:T(2,128)S(1)} %bitcast.34), kind=kOutput, calls=%fused_computation.11.clone.1 | convolution fusion | flops 64225280 | bytes 5410817 | tf_op jit(solution)/shard_map/while/body/eval_jaxpr/rkf,kgh->grhf/dot_general | solution.py:56
  136.0 8.3 %fusion.32 = bf16[8,8192,64]{1,2,0:T(8,128)(2,1)S(1)} fusion(s32[64]{0:T(128)S(1)} %iota_multiply_fusion.4, s32[8192]{0:T(1024)S(1)} %iota_multiply_fusion.5, s32[8]{0:T(128)S(1)} %select_reduce_fusion.2), kind=kLoop, calls=%fused_computation.10.clone.1 | loop fusion | flops 67108864 | bytes 8421664 | tf_op jit(solution)/shard_map/while/body/eval_jaxpr/convert_element_type | solution.py:51
  144.3 3.7 %fusion.33 = f32[80,512]{0,1:S(1)} fusion(bf16[8192,512]{0,1:T(8,128)(2,1)S(1)} %bitcast.31, bf16[80,65536]{1,0:T(8,128)(2,1)} %get-tuple-element.292, s32[]{:T(128)S(6)} %select_n.16), kind=kOutput, calls=%fused_computation.12.clone.1 | convolution fusion | flops 671088640 | bytes 9961476 | tf_op jit(solution)/shard_map/while
  148.0 6.6 %bitcast_add_fusion.2 = f32[64,80,2,64]{1,0,3,2:T(8,128)} fusion(f32[64,80,2,64]{1,0,3,2:T(8,128)} %get-tuple-element.279, pred[]{:T(512)S(6)} %compare.3, f32[80,8,64]{0,2,1:T(8,128)S(1)} %bitcast.33, f32[8,64,2,1]{0,2,1,3:T(2,128)S(1)} %bitcast.34), kind=kOutput, calls=%fused_computation.11.clone.1 | convolution fusion | flops 64225280 | bytes 5410817 | tf_op jit(solution)/shard_map/while/body/eval_jaxpr/rkf,kgh->grhf/dot_general | solution.py:56
  154.7 8.3 %fusion.32 = bf16[8,8192,64]{1,2,0:T(8,128)(2,1)S(1)} fusion(s32[64]{0:T(128)S(1)} %iota_multiply_fusion.4, s32[8192]{0:T(1024)S(1)} %iota_multiply_fusion.5, s32[8]{0:T(128)S(1)} %select_reduce_fusion.2), kind=kLoop, calls=%fused_computation.10.clone.1 | loop fusion | flops 67108864 | bytes 8421664 | tf_op jit(solution)/shard_map/while/body/eval_jaxpr/convert_element_type | solution.py:51
  163.1 3.7 %fusion.33 = f32[80,512]{0,1:S(1)} fusion(bf16[8192,512]{0,1:T(8,128)(2,1)S(1)} %bitcast.31, bf16[80,65536]{1,0:T(8,128)(2,1)} %get-tuple-element.292, s32[]{:T(128)S(6)} %select_n.16), kind=kOutput, calls=%fused_computation.12.clone.1 | convolution fusion | flops 671088640 | bytes 9961476 | tf_op jit(solution)/shard_map/while
  166.8 6.6 %bitcast_add_fusion.2 = f32[64,80,2,64]{1,0,3,2:T(8,128)} fusion(f32[64,80,2,64]{1,0,3,2:T(8,128)} %get-tuple-element.279, pred[]{:T(512)S(6)} %compare.3, f32[80,8,64]{0,2,1:T(8,128)S(1)} %bitcast.33, f32[8,64,2,1]{0,2,1,3:T(2,128)S(1)} %bitcast.34), kind=kOutput, calls=%fused_computation.11.clone.1 | convolution fusion | flops 64225280 | bytes 5410817 | tf_op jit(solution)/shard_map/while/body/eval_jaxpr/rkf,kgh->grhf/dot_general | solution.py:56
  173.4 5.2 %copy.43 = f32[64,80,128]{2,1,0:T(8,128)} copy(f32[64,80,128]{1,0,2:T(8,128)} %bitcast.32) | data formatting | bytes 5242880 | tf_op jit(solution)/shard_map/reshape | solution.py:63
  178.6 0.0 reduce-scatter.2.cloned.1.call-update
  178.6 79.4 %reduce-scatter.2.cloned.1.call-done = f32[4,80,128]{2,1,0:T(8,128)} async-done(((f32[64,80,128]{2,1,0:T(8,128)}), f32[4,80,128]{2,1,0:T(8,128)}) %reduce-scatter.2.cloned.1.call-update) | async-done | bytes 163856 | tf_op jit(solution)/shard_map/reduce_scatter | solution.py:62
  258.0 1.0 multiply_reduce_fusion
  259.0 0.9 multiply_reduce_fusion.1
  259.9 32.8 %all-reduce = (f32[16]{0:T(128)S(1)}, f32[64]{0:T(128)S(1)}) all-reduce(f32[16]{0:T(128)S(1)} %multiply_reduce_fusion.1, f32[64]{0:T(128)S(1)} %multiply_reduce_fusion), channel_id=1, replica_groups=mesh['feat'=16,'cand'=16] {'feat'}, use_global_device_ids=true, to_apply=%region_5.0 | all-reduce | flops 80 | bytes 640 | tf_op jit(solution)/shard_map/psum | solution.py:67
  292.7 0.8 slice_divide_fusion
  293.5 25.5 %all_gather.7 = f32[4,256,128]{2,1,0:T(8,128)S(1)} all-gather(f32[4,16,128]{2,1,0:T(8,128)S(1)} %slice_divide_fusion), channel_id=1, replica_groups=mesh['feat'=16,'cand'=16] {'cand'}, dimensions={1}, use_global_device_ids=true | all-gather | bytes 557056 | tf_op jit(solution)/shard_map/all_gather | solution.py:69
  319.1 1.5 fusion.18
  320.5 0.1 reduce_sum.53
  320.6 0.1 copy.45
  320.7 32.4 %all-gather = f32[1024,64]{1,0:T(8,128)S(1)} all-gather(f32[64,64]{1,0:T(8,128)S(1)} %copy.45), channel_id=2, replica_groups=mesh['feat'=16,'cand'=16] {'feat'}, dimensions={0}, use_global_device_ids=true | all-gather | bytes 278528 | tf_op jit(solution)/shard_map/all_gather | solution.py:72
  353.2 0.1 constant_dynamic-slice_fusion
  353.3 0.1 copy.54
  353.4 0.6 broadcast_divide_fusion
  (37 shorter events, 0.6 us)
Async XLA Ops:
  6.5 12.2 %copy-start = (bf16[16,65536]{1,0:T(8,128)(2,1)S(1)}, bf16[16,65536]{1,0:T(8,128)(2,1)}, u32[]{:S(2)}) copy-start(bf16[16,65536]{1,0:T(8,128)(2,1)} %param.8) | copy-start | bytes 6291460
  6.5 251.5 %reduce-scatter.2.cloned.1.call-start = ((), (), s32[]{:S(2)}) async-start(), calls=%async_computation.1 | async-start | bytes 2785280 | tf_op jit(solution)/shard_map/reduce_scatter | solution.py:62
Sparse Core Ops, SparseCore 0:
  178.7 79.2 reduce-scatter.1
